TPU v7x, 32 devices: a whole 2x2x4 slice. The times are simulated.
32 devices in a mesh: area: 8 (over z, x), row: 4 (over y, core).
Axes of the slice: x: 2, y: 2, z: 4, core: 2. Of those that a mesh axis runs over, the one named last changes fastest.
Arguments:
- conductance_inverse: float32 [32, 1024, 1024], P(('area', 'row')), as said below
- cap_history: float32 [32, 1024, 128], P(('area', 'row')), may hold values from -3 to 3
- cap_conductance: float32 [32, 1024], P(('area', 'row')), may hold values from 0.5 to 0.8
- wave_history: float32 [32, 40, 32, 128], P(('area', 'row')), may hold values from -6 to 6
- line_partner: int32 [32, 32], P(('area', 'row')), may hold values from 0 to 31, as said below
- line_node: int32 [32, 32], P(('area', 'row')), may hold values from 0 to 1023
- line_delay: int32 [32, 32], P(('area', 'row')), may hold values from 20 to 40
- line_admittance: float32 [32, 32], P(('area', 'row')), may hold values from 0.2 to 1
- conv_node: int32 [32, 64], P(('area', 'row')), may hold values from 0 to 1023
- conv_count: int32 [32], P(('area', 'row')), may hold values from 1 to 64, as said below
- conv_state: float32 [32, 2, 64, 128], P(('area', 'row')), may hold values from -3 to 3
- conv_reference: float32 [32, 2, 64, 128], P(('area', 'row')), may hold values from -4 to 4
- conv_rate: float32 [32, 64], P(('area', 'row')), may hold values from 0.03 to 0.6
- conv_limit: float32 [32, 64], P(('area', 'row')), may hold values from 1 to 2.5
- port_node: int32 [32, 8], P(('area', 'row')), may hold values from 0 to 1023
- port_admittance: float32 [32, 8], P(('area', 'row')), may hold values from 0.3 to 1.2
- port_voltage_prev: float32 [2, 32, 8, 128], P(None, ('area', 'row')), may hold values from -5 to 5
- port_bus: int32 [32, 8], P('area'), may hold values from 0 to 20479
- transfer_impedance: float32 [2, 20480, 256], P(None, 'row', 'area'), may hold values from -0.75 to 0.75
Outputs:
- waves: float32 [32, 20, 32, 128], P(('area', 'row'))
- cap_history_out: float32 [32, 1024, 128], P(('area', 'row'))
- conv_state_out: float32 [32, 2, 64, 128], P(('area', 'row'))
- bus_voltage: float32 [2, 20480, 128], P(None, 'row')
- port_voltage: float32 [2, 32, 8, 128], P(None, ('area', 'row'))
Inputs may be any that keep to these rules, and one draw needn't show every extreme that they name: Slot l < 16 of subnetwork s and slot l + 16 of subnetwork (s + k_l) mod 32 are the two ends of one line, with k_l in 1 or 2 the same for every subnetwork and exactly 12 of the k_l equal to 1; so line_partner[s, l] = (s + k_l) mod 32 and line_partner[s, l + 16] = (s - k_l) mod 32. `conv_count`: some subnetwork has all 64 converters in service. `conductance_inverse`: each subnetwork's inverse nodal conductance matrix.
All inputs are finite; a program needn't handle non-finite values.
Results may differ from a plain program's by a relative error of at most 0.0003.
Values sent between devices are 32-bit elements; how exact they have to be, the bound alone decides.
A program may use at most 64 MiB of HBM per device.

v0:
```python
import functools
import math

import jax
import jax.numpy as jnp
from jax import lax
from jax.experimental import pallas as pl
from jax.experimental.pallas import tpu as pltpu
from jax.sharding import PartitionSpec as P

STEPS = 20
HIST = 40
SAG_FACTOR = 0.3
F32 = jnp.float32
BF16 = jnp.bfloat16
MESH = pl.DeviceIdType.MESH


def shifted(x, by):
    axes = ("area", "row")
    size = lax.axis_size(axes)
    return lax.ppermute(x, axes, [(i, (i + by) % size) for i in range(size)])


def split(x):
    high = x.astype(BF16)
    return high, (x - high.astype(F32)).astype(BF16)


def mm(a, b):
    return lax.dot_general(a, b, (((1,), (0,)), ((), ())), preferred_element_type=F32)


def columns(row, count):
    return jnp.broadcast_to(row, (128, count)).T


def window_kernel(
    lines,
    convs,
    ports,
    reach_ref,
    delay_ref,
    trig_ref,
    count_ref,
    index_ref,
    coef_ref,
    ginv_ref,
    gcap_ref,
    hist_ref,
    below1_ref,
    below2_ref,
    above1_ref,
    above2_ref,
    state_ref,
    target_ref,
    pvolt_ref,
    zc_ref,
    waves_ref,
    hist_out_ref,
    state_out_ref,
    flat_ref,
    bus_ref,
    big,
    wj,
    wx,
    cap2,
    xs,
    current_ref,
    zin,
    cin,
    mine,
    rh,
    rl,
    zs,
    zr,
    rs,
    rr,
    cs,
    cr,
    zlocal,
    os,
    orr,
    fs,
    fr,
    olocal,
):
    nodes = ginv_ref.shape[0]
    probes = 128
    half = lines // 2
    rows = 256
    areas, group = cin.shape[0], cin.shape[1]
    depth, chunk = zin.shape[1], zin.shape[2]
    a = lax.axis_index("area")
    r = lax.axis_index("row")

    barrier = pltpu.get_barrier_semaphore()
    for d in range(1, areas):
        pl.semaphore_signal(barrier, inc=1, device_id=(lax.rem(a + d, areas), r), device_id_type=MESH)
    for d in range(1, group):
        pl.semaphore_signal(barrier, inc=1, device_id=(a, lax.rem(r + d, group)), device_id_type=MESH)
    pl.semaphore_wait(barrier, areas + group - 2)

    def send(src, dst, ssem, rsem, to):
        return pltpu.make_async_remote_copy(
            src_ref=src, dst_ref=dst, send_sem=ssem, recv_sem=rsem, device_id=to, device_id_type=MESH
        )

    own_z = pltpu.make_async_copy(zc_ref.at[a], zin.at[a], zlocal)
    own_z.start()
    z_copies = []
    for d in range(1, areas):
        to = lax.rem(a + d, areas)
        copy = send(zc_ref.at[to], zin.at[a], zs.at[d], zr.at[d], (to, r))
        copy.start()
        z_copies.append(copy)

    index = columns(index_ref[...].astype(F32), probes).astype(jnp.int32)
    for c in range(nodes // 128):
        lane = lax.broadcasted_iota(jnp.int32, (probes, 128), 1) + 128 * c
        cap2[:, c * 128 : (c + 1) * 128] = jnp.where(index == lane, 1.0, 0.0)
    pick = cap2[...].astype(BF16)
    scatter = cap2[...].T.astype(BF16)
    for b in range(nodes // rows):
        span = pl.ds(b * rows, rows)
        high, low = split(ginv_ref[span, :])
        big[span, 0:nodes] = high
        big[span, nodes : 2 * nodes] = low
    tail = pl.ds(nodes, probes)
    big[tail, :nodes] = mm(pick, big[0:nodes, 0:nodes]).astype(BF16)
    big[tail, nodes : 2 * nodes] = mm(pick, big[0:nodes, nodes : 2 * nodes]).astype(BF16)
    big[:, 2 * nodes : 2 * nodes + 128] = mm(big[:, 0:nodes], scatter).astype(BF16)
    big[:, 2 * nodes + 128 :] = mm(big[:, nodes : 2 * nodes], scatter).astype(BF16)
    gcap = 2.0 * columns(gcap_ref[...], nodes)

    def put_state(value):
        high, low = split(value)
        wj[:, 0:128] = high
        wj[:, 128:256] = low

    hist_out_ref[...] = hist_ref[...]
    put_state(hist_ref[...])
    state_out_ref[...] = state_ref[...]
    current_ref[...] = jnp.zeros_like(current_ref)
    coef = coef_ref[...]
    two_adm = columns(coef[0:1], 128)[0:lines]
    rate = columns(coef[1:2], 128)[lines : lines + convs]
    limit = columns(coef[2:3], 128)[lines : lines + convs]
    padm = columns(coef[0:1], 128)[lines + convs : lines + convs + ports]
    live = lax.broadcasted_iota(jnp.int32, (convs, 128), 0) < count_ref[0]
    xs[lines + convs + ports :, :] = jnp.zeros((probes - lines - convs - ports, 128), F32)

    def step(t, carry):
        cosine = trig_ref[0, t]
        sine = trig_ref[1, t]
        for l in range(half):
            up = jnp.clip(t - delay_ref[l] + HIST, 0, HIST - 1)
            down = jnp.clip(t - delay_ref[l + half] + HIST, 0, HIST - 1)
            near = reach_ref[l] == 1
            xs[l : l + 1, :] = jnp.where(near, above1_ref[up, l : l + 1, :], above2_ref[up, l : l + 1, :])
            xs[l + half : l + half + 1, :] = jnp.where(
                near, below1_ref[down, l : l + 1, :], below2_ref[down, l : l + 1, :]
            )
        inward = xs[0:lines, :]
        axial = state_out_ref[0]
        normal = state_out_ref[1]
        source = padm * (pvolt_ref[0] * cosine - pvolt_ref[1] * sine)
        xs[lines : lines + convs, :] = jnp.where(live, axial * cosine - normal * sine, 0.0)
        xs[lines + convs : lines + convs + ports, :] = source
        high, low = split(xs[...])
        wx[0:128, 0:128] = high
        wx[128:256, 0:128] = high
        wx[0:128, 128:256] = low
        wx[128:256, 128:256] = low

        def apply(start, size):
            span = pl.ds(start, size)
            both = (
                mm(big[span, 0:nodes], wj[...])
                + mm(big[span, nodes : 2 * nodes], wj[...])
                + mm(big[span, 2 * nodes :], wx[...])
            )
            return both[:, 0:128] + both[:, 128:256]

        probe = apply(nodes, probes)
        volts = apply(0, nodes)
        waves_ref[t] = two_adm * probe[0:lines] - inward
        emf = probe[lines : lines + convs]
        flow = source - padm * probe[lines + convs : lines + convs + ports]
        current_ref[0] += flow * cosine
        current_ref[1] -= flow * sine
        new_axial = axial + rate * (target_ref[0] - axial) - SAG_FACTOR * emf * cosine
        new_normal = normal + rate * (target_ref[1] - normal) + SAG_FACTOR * emf * sine
        state_out_ref[0] = jnp.where(live, limit * jnp.tanh(new_axial / limit), axial)
        state_out_ref[1] = jnp.where(live, limit * jnp.tanh(new_normal / limit), normal)
        after = gcap * volts - hist_out_ref[...]
        hist_out_ref[...] = after
        put_state(after)
        return carry

    lax.fori_loop(0, STEPS, step, 0)
    cin[a, r] = current_ref[...] * (2.0 / STEPS)

    copies = []
    for d in range(1, group):
        block = cin.at[a, r]
        copy = send(block, block, rs.at[d], rr.at[d], (a, lax.rem(r + d, group)))
        copy.start()
        copies.append(copy)
    for copy in copies:
        copy.wait()
    copies = []
    for d in range(1, areas):
        block = cin.at[a]
        copy = send(block, block, cs.at[d], cr.at[d], (lax.rem(a + d, areas), r))
        copy.start()
        copies.append(copy)
    own_z.wait()
    for copy in z_copies:
        copy.wait()
    for copy in copies:
        copy.wait()
    members = group * ports
    for i in range(areas):
        for j in range(group):
            re, im = cin[i, j, 0], cin[i, j, 1]
            top = i * depth + j * ports
            flat_ref[top : top + ports, 0:128] = re
            flat_ref[top : top + ports, 128:256] = im
            flat_ref[top + members : top + members + ports, 0:128] = -im
            flat_ref[top + members : top + members + ports, 128:256] = re
    high, low = split(flat_ref[...])
    rh[...] = high
    rl[...] = low
    high, low = split(zin[...].reshape(areas * depth, chunk).T)
    total = mm(high, rh[...]) + mm(low, rh[...]) + mm(high, rl[...])
    mine[0] = total[:, 0:128]
    mine[1] = total[:, 128:256]

    inner = 2 ** ((areas.bit_length() - 1) // 2)
    outer = areas // inner
    zi = lax.div(a, inner)
    xi = lax.rem(a, inner)

    def region(part, who):
        return bus_ref.at[part, pl.ds(pl.multiple_of(who * chunk, 8), chunk), :]

    pending = []
    arrivals = []
    for part in range(2):
        local = pltpu.make_async_copy(mine.at[part], region(part, a), olocal.at[part])
        local.start()
        pending.append(local)
        for d in range(1, inner):
            to = zi * inner + lax.rem(xi + d, inner)
            k = part * areas + d
            copy = send(mine.at[part], region(part, a), os.at[k], orr.at[k], (to, r))
            copy.start()
            pending.append(copy)
        for d in range(1, outer):
            to = lax.rem(zi + d, outer) * inner + xi
            k = part * areas + inner * d
            copy = send(mine.at[part], region(part, a), os.at[k], orr.at[k], (to, r))
            copy.start()
            arrivals.append((part, d, copy))
    for part, d, copy in arrivals:
        copy.wait_recv()
        source = lax.rem(zi + outer - d, outer) * inner + xi
        for e in range(1, inner):
            to = zi * inner + lax.rem(xi + e, inner)
            k = part * areas + inner * d + e
            block = region(part, source)
            forward = send(block, block, fs.at[k], fr.at[k], (to, r))
            forward.start()
            pending.append(forward)
    for _, _, copy in arrivals:
        copy.wait_send()
    for copy in pending:
        copy.wait()


def vmem():
    return pl.BlockSpec(memory_space=pltpu.VMEM)


def smem():
    return pl.BlockSpec(memory_space=pltpu.SMEM)


def per_device(
    conductance_inverse,
    cap_history,
    cap_conductance,
    wave_history,
    line_partner,
    line_node,
    line_delay,
    line_admittance,
    conv_node,
    conv_count,
    conv_state,
    conv_reference,
    conv_rate,
    conv_limit,
    port_node,
    port_admittance,
    port_voltage_prev,
    port_bus,
    transfer_impedance,
):
    subnets = lax.axis_size(("area", "row"))
    own = lax.axis_index(("area", "row"))
    history = wave_history[0]
    lines = history.shape[1]
    half = lines // 2
    cases = history.shape[2]
    nodes = conductance_inverse.shape[1]
    convs = conv_node.shape[1]
    ports = port_node.shape[1]
    upper = history[:, :half]
    lower = history[:, half:]
    below1 = shifted(upper, 1)
    above1 = shifted(lower, -1)
    below2 = shifted(upper, 2)
    above2 = shifted(lower, -2)
    reach = (line_partner[0] - own) % subnets
    areas = lax.axis_size("area")
    group = lax.axis_size("row")
    bus_rows = transfer_impedance.shape[1]
    members = transfer_impedance.shape[2]
    chunk = bus_rows // areas
    zt = jnp.transpose(transfer_impedance, (0, 2, 1)).reshape(2 * members, bus_rows)
    zc = jnp.transpose(zt.reshape(2 * members, areas, chunk), (1, 0, 2))

    pad = 128 - lines - convs - ports
    index = jnp.concatenate([line_node, conv_node, port_node, jnp.full((1, pad), -1, jnp.int32)], axis=1)
    ones = jnp.ones((1, 128 - lines - convs), F32)
    coef = jnp.concatenate(
        [
            jnp.concatenate([2.0 * line_admittance, jnp.ones((1, convs), F32), port_admittance, ones[:, :pad]], axis=1),
            jnp.concatenate([jnp.ones((1, lines), F32), conv_rate, ones], axis=1),
            jnp.concatenate([jnp.ones((1, lines), F32), conv_limit, ones], axis=1),
        ],
        axis=0,
    )
    angles = jnp.arange(1, STEPS + 1, dtype=F32) * jnp.float32(2.0 * math.pi / STEPS)
    trig = jnp.stack([jnp.cos(angles), jnp.sin(angles)])
    flops = 2 * STEPS * (nodes + 128) * (2 * nodes + 256) * 256
    waves, hist_end, conv_out, _, bus_voltage = pl.pallas_call(
        functools.partial(window_kernel, lines, convs, ports),
        out_shape=(
            jax.ShapeDtypeStruct((STEPS, lines, cases), F32),
            jax.ShapeDtypeStruct((nodes, cases), F32),
            jax.ShapeDtypeStruct((2, convs, cases), F32),
            jax.ShapeDtypeStruct((areas * 2 * members, 2 * cases), F32),
            jax.ShapeDtypeStruct((2, bus_rows, cases), F32),
        ),
        in_specs=[smem()] * 4 + [vmem()] * 12 + [pl.BlockSpec(memory_space=pl.ANY)],
        out_specs=(vmem(),) * 4 + (pl.BlockSpec(memory_space=pl.ANY),),
        scratch_shapes=[
            pltpu.VMEM((nodes + 128, 2 * nodes + 256), BF16),
            pltpu.VMEM((nodes, 256), BF16),
            pltpu.VMEM((256, 256), BF16),
            pltpu.VMEM((128, nodes), F32),
            pltpu.VMEM((128, 128), F32),
            pltpu.VMEM((2, ports, cases), F32),
            pltpu.VMEM((areas, 2 * members, chunk), F32),
            pltpu.VMEM((areas, group, 2, ports, cases), F32),
            pltpu.VMEM((2, chunk, cases), F32),
            pltpu.VMEM((areas * 2 * members, 2 * cases), BF16),
            pltpu.VMEM((areas * 2 * members, 2 * cases), BF16),
            pltpu.SemaphoreType.DMA((areas,)),
            pltpu.SemaphoreType.DMA((areas,)),
            pltpu.SemaphoreType.DMA((group,)),
            pltpu.SemaphoreType.DMA((group,)),
            pltpu.SemaphoreType.DMA((areas,)),
            pltpu.SemaphoreType.DMA((areas,)),
            pltpu.SemaphoreType.DMA,
            pltpu.SemaphoreType.DMA((2 * areas,)),
            pltpu.SemaphoreType.DMA((2 * areas,)),
            pltpu.SemaphoreType.DMA((2 * areas,)),
            pltpu.SemaphoreType.DMA((2 * areas,)),
            pltpu.SemaphoreType.DMA((2,)),
        ],
        compiler_params=pltpu.CompilerParams(collective_id=0, has_side_effects=True),
        cost_estimate=pl.CostEstimate(flops=flops, bytes_accessed=8_000_000, transcendentals=0),
        name="window",
    )(
        reach,
        line_delay[0],
        trig,
        conv_count,
        index,
        coef,
        conductance_inverse[0],
        cap_conductance,
        cap_history[0],
        below1,
        below2,
        above1,
        above2,
        conv_state[0],
        conv_reference[0],
        port_voltage_prev[:, 0],
        zc,
    )

    local = port_bus.reshape(-1) - lax.axis_index("row") * bus_rows
    inside = (local >= 0) & (local < bus_rows)
    local = jnp.clip(local, 0, bus_rows - 1)
    chosen = jnp.concatenate([local, local + bus_rows])
    taken = jnp.take(bus_voltage.reshape(2 * bus_rows, cases), chosen, axis=0, mode="clip")
    taken = jnp.where(jnp.concatenate([inside, inside])[:, None], taken, 0.0)
    taken = taken.reshape(2, port_bus.shape[0], port_bus.shape[1], cases)
    port_voltage = lax.psum_scatter(taken, "row", scatter_dimension=1, tiled=True)
    return (waves[None], hist_end[None], conv_out[None], bus_voltage, port_voltage)


def solution(mesh):
    both = ("area", "row")
    placed = (
        P(both, None, None),
        P(both, None, None),
        P(both, None),
        P(both, None, None, None),
        P(both, None),
        P(both, None),
        P(both, None),
        P(both, None),
        P(both, None),
        P(both),
        P(both, None, None, None),
        P(both, None, None, None),
        P(both, None),
        P(both, None),
        P(both, None),
        P(both, None),
        P(None, both, None, None),
        P("area", None),
        P(None, "row", "area"),
    )
    return jax.shard_map(
        per_device,
        mesh=mesh,
        in_specs=placed,
        out_specs=(
            P(both, None, None, None),
            P(both, None, None),
            P(both, None, None, None),
            P(None, "row", None),
            P(None, both, None, None),
        ),
        check_vma=False,
    )
```

profile of v0, /device:TPU:16, one launch (start us, length us, event | category | flops | bytes accessed | tf_op | source)
XLA Modules:
  0.0 180.7 jit_solution(17011591792037738066)
XLA Ops:
  0.6 0.0 copy-start.11
  0.7 1.2 fusion.3
  1.9 2.4 %collective-permute-start.3 = (f32[40,16,128]{2,1,0:T(8,128)S(1)}, f32[40,16,128]{2,1,0:T(8,128)S(1)}, u32[]{:S(2)}, u32[]{:S(2)}) collective-permute-start(f32[40,16,128]{2,1,0:T(8,128)S(1)} %get-tuple-element.13), channel_id=1, source_target_pairs={{0,30},{1,31},{2,0},{3,1},{4,2},{5,3},{6,4},{7,5},{8,6},{9,7},{10,... | collective-permute-start | bytes 983048 | tf_op jit(solution)/shard_map/ppermute | solution.py:22
  4.3 1.2 collective-permute-start.1
  5.5 0.7 and_bitcast_fusion
  6.2 0.7 subtract_clamp_fusion
  7.5 0.7 broadcast_multiply_fusion
  8.2 0.1 min.12
  8.3 0.1 pad_add_fusion.1
  8.4 1.6 copy.28
  9.9 1.3 copy.30
  11.2 0.6 dynamic-slice
  11.9 0.6 pad_maximum_fusion.trig_ref
  12.5 0.7 maximum_maximum_fusion.coef_ref
  13.2 0.6 bitcast_add_fusion.index_ref
  13.8 0.5 and_select_fusion.reach_ref
  14.3 7.6 %collective-permute-done.3.above2_ref = f32[40,16,128]{2,1,0:T(8,128)S(1)} collective-permute-done((f32[40,16,128]{2,1,0:T(8,128)S(1)}, f32[40,16,128]{2,1,0:T(8,128)S(1)}, u32[]{:S(2)}, u32[]{:S(2)}) %collective-permute-start.3) | collective-permute-done | bytes 327712 | tf_op jit(solution)/shard_map/ppermute | solution.py:22
  21.9 0.0 collective-permute-done.1.below2_ref
  22.0 0.0 copy-start.9
  22.0 0.7 copy-done.6
  22.7 0.1 copy-done.7
  22.8 0.1 copy-done.8
  22.9 0.1 copy-done.9
  23.0 132.8 %window.1 = (f32[20,32,128]{2,1,0:T(8,128)}, f32[1024,128]{1,0:T(8,128)}, f32[2,64,128]{2,1,0:T(8,128)}, f32[512,256]{1,0:T(8,128)}, f32[2,5120,128]{2,1,0:T(8,128)}) custom-call(s32[32]{0:T(128)} %and_select_fusion.reach_ref, s32[32]{0:T(128)} %bitcast.42, f32[2,20]{1,0:T(2,128)} %pad_maximum_fusion.trig_ref, s32[1]{0:T(128)S(6)} %copy.35.count_ref, ...), custom_call_target="tpu_custom_call" | custom-call | flops 27179089920 | bytes 8000000 | tf_op jit(solution)/shard_map/window/pallas_call | solution.py:349
  155.8 3.1 %gather_fusion = f32[64,128]{1,0:T(8,128)S(1)} fusion(f32[10240,128]{1,0:T(8,128)} %bitcast.28, s32[1024]{0:T(1024)S(1)} %pad_clamp_fusion), kind=kCustom, calls=%fused_computation | custom fusion | bytes 65792 | tf_op jit(solution)/shard_map/jit(_take)/gather | solution.py:412
  158.9 0.1 broadcast_select_fusion
  159.0 10.3 %all-reduce = f32[2,4,8,128]{3,2,1,0:T(8,128)S(1)} all-reduce(f32[2,4,8,128]{3,2,1,0:T(8,128)S(1)} %broadcast_select_fusion), channel_id=2, replica_groups=mesh['area'=8,'row'=4] {'row'}, use_global_device_ids=true, to_apply=%region_0.1.clone | all-reduce | flops 8192 | bytes 65536
  169.2 1.2 constant_dynamic-slice_fusion
  170.5 1.7 copy.36
  172.2 1.9 %copy.37 = f32[1,1024,128]{2,1,0:T(8,128)} copy(f32[1,1024,128]{2,1,0:T(8,128)} %bitcast.33) | data formatting | bytes 1048576
  174.0 1.5 copy.38
  175.5 5.2 %copy.39 = f32[2,5120,128]{2,1,0:T(8,128)} copy(f32[2,5120,128]{2,1,0:T(8,128)} %get-tuple-element.25) | data formatting | bytes 10485760
  (30 shorter events, 0.1 us)
Async XLA Ops:
  0.6 10.6 %copy-start.11 = (u32[32]{0:T(128)S(1)}, u32[32]{0:T(128)}, u32[]{:S(2)}) copy-start(u32[32]{0:T(128)} %constant.66) | copy-start | bytes 388
  0.6 11.8 %copy-start.5 = (f32[1,8]{1,0:T(1,128)S(1)}, f32[1,8]{1,0:T(1,128)}, u32[]{:S(2)}) copy-start(f32[1,8]{1,0:T(1,128)} %param.34) | copy-start | bytes 100
  0.7 11.8 %copy-start.3 = (f32[1,64]{1,0:T(1,128)S(1)}, f32[1,64]{1,0:T(1,128)}, u32[]{:S(2)}) copy-start(f32[1,64]{1,0:T(1,128)} %param.32) | copy-start | bytes 772
  0.7 11.8 %copy-start.4 = (f32[1,64]{1,0:T(1,128)S(1)}, f32[1,64]{1,0:T(1,128)}, u32[]{:S(2)}) copy-start(f32[1,64]{1,0:T(1,128)} %param.31) | copy-start | bytes 772
  0.7 12.5 %copy-start = (s32[1,8]{1,0:T(1,128)S(1)}, s32[1,8]{1,0:T(1,128)}, u32[]{:S(2)}) copy-start(s32[1,8]{1,0:T(1,128)} %param.33) | copy-start | bytes 100
  0.7 12.5 %copy-start.1 = (s32[1,64]{1,0:T(1,128)S(1)}, s32[1,64]{1,0:T(1,128)}, u32[]{:S(2)}) copy-start(s32[1,64]{1,0:T(1,128)} %param.27) | copy-start | bytes 772
  0.7 12.5 %copy-start.2 = (s32[1,32]{1,0:T(1,128)S(1)}, s32[1,32]{1,0:T(1,128)}, u32[]{:S(2)}) copy-start(s32[1,32]{1,0:T(1,128)} %param.24) | copy-start | bytes 388
  0.7 13.0 %copy-start.10 = (s32[1,32]{1,0:T(1,128)S(1)}, s32[1,32]{1,0:T(1,128)}, u32[]{:S(2)}) copy-start(s32[1,32]{1,0:T(1,128)} %param.23) | copy-start | bytes 388
  1.9 20.0 %collective-permute-start.3 = (f32[40,16,128]{2,1,0:T(8,128)S(1)}, f32[40,16,128]{2,1,0:T(8,128)S(1)}, u32[]{:S(2)}, u32[]{:S(2)}) collective-permute-start(f32[40,16,128]{2,1,0:T(8,128)S(1)} %get-tuple-element.13), channel_id=1, source_target_pairs={{0,30},{1,31},{2,0},{3,1},{4,2},{5,3},{6,4},{7,5},{8,6},{9,7},{10,... | collective-permute-start | bytes 983048 | tf_op jit(solution)/shard_map/ppermute | solution.py:22
  4.3 17.7 %collective-permute-start.2 = (f32[40,16,128]{2,1,0:T(8,128)S(1)}, f32[40,16,128]{2,1,0:T(8,128)S(1)}, u32[]{:S(2)}, u32[]{:S(2)}) collective-permute-start(f32[40,16,128]{2,1,0:T(8,128)S(1)} %get-tuple-element.13), channel_id=1, source_target_pairs={{0,31},{1,0},{2,1},{3,2},{4,3},{5,4},{6,5},{7,6},{8,7},{9,8},{10,9... | collective-permute-start | bytes 983048 | tf_op jit(solution)/shard_map/ppermute | solution.py:22
  4.3 17.7 %collective-permute-start.1 = (f32[40,16,128]{2,1,0:T(8,128)S(1)}, f32[40,16,128]{2,1,0:T(8,128)S(1)}, u32[]{:S(2)}, u32[]{:S(2)}) collective-permute-start(f32[40,16,128]{2,1,0:T(8,128)S(1)} %get-tuple-element.14), channel_id=1, source_target_pairs={{0,2},{1,3},{2,4},{3,5},{4,6},{5,7},{6,8},{7,9},{8,10},{9,11},{10,... | collective-permute-start | bytes 983048 | tf_op jit(solution)/shard_map/ppermute | solution.py:22
  5.5 16.5 %collective-permute-start = (f32[40,16,128]{2,1,0:T(8,128)S(1)}, f32[40,16,128]{2,1,0:T(8,128)S(1)}, u32[]{:S(2)}, u32[]{:S(2)}) collective-permute-start(f32[40,16,128]{2,1,0:T(8,128)S(1)} %get-tuple-element.14), channel_id=1, source_target_pairs={{0,1},{1,2},{2,3},{3,4},{4,5},{5,6},{6,7},{7,8},{8,9},{9,10},{10,1... | collective-permute-start | bytes 983048 | tf_op jit(solution)/shard_map/ppermute | solution.py:22
  21.9 0.7 copy-start.6
  21.9 0.8 copy-start.7
  22.0 0.9 copy-start.8
  22.0 1.0 copy-start.9
where the time goes:
time: 181 us
  Pallas kernels  133 us (73%)
  local copies, waits for them, and re-layouts  20.3 us (11%)
  blocking collectives  10.3 us (6%)
  waiting for transfers between devices  7.66 us (4%)
  other arithmetic  4.63 us (3%)
  starting transfers between devices  3.57 us (2%)
    pallas_call x1, Pallas kernels, per_device(): pl.pallas_call(functools.partial(window_kernel, lines, convs, ports), out...  133 us
    unnamed x31, local copies, waits for them, and re-layouts  14.7 us
    unnamed x1, blocking collectives  10.3 us
    ppermute x4, waiting for transfers between devices, shifted(): return lax.ppermute(x, axes, [(i, (i + by) % size) for i in range(size)])  7.66 us
  transfers between devices with their start and end apart: 4, of which 1 were waited for; matrix products, arithmetic and copies ran while one was open for 4% of the time, Pallas kernels for 0%

commit v1 on v0

--- a/solution.py
+++ b/solution.py
@@ -14,6 +14,7 @@
 F32 = jnp.float32
 BF16 = jnp.bfloat16
 MESH = pl.DeviceIdType.MESH
+SUBS = 10
 
 
 def shifted(x, by):
@@ -55,11 +56,12 @@
     state_ref,
     target_ref,
     pvolt_ref,
+    port_bus_ref,
     zc_ref,
     waves_ref,
     hist_out_ref,
     state_out_ref,
-    flat_ref,
+    port_ref,
     bus_ref,
     big,
     wj,
@@ -69,11 +71,13 @@
     current_ref,
     zin,
     cin,
-    mine,
+    vbus,
+    flat_ref,
     rh,
     rl,
     zs,
     zr,
+    zf,
     rs,
     rr,
     cs,
@@ -82,17 +86,28 @@
     os,
     orr,
     fs,
-    fr,
+    xf,
+    xr,
     olocal,
+    picked,
+    landed,
+    ps,
+    pr,
 ):
     nodes = ginv_ref.shape[0]
     probes = 128
     half = lines // 2
     rows = 256
     areas, group = cin.shape[0], cin.shape[1]
-    depth, chunk = zin.shape[1], zin.shape[2]
+    pieces, depth, width = zin.shape[0], zin.shape[2], zin.shape[3]
+    inner = 2 ** ((areas.bit_length() - 1) // 2)
+    outer = areas // inner
+    span_rows = bus_ref.shape[1] // outer
+    chunk = span_rows // inner
     a = lax.axis_index("area")
     r = lax.axis_index("row")
+    zi = lax.div(a, inner)
+    xi = lax.rem(a, inner)
 
     barrier = pltpu.get_barrier_semaphore()
     for d in range(1, areas):
@@ -106,14 +121,37 @@
             src_ref=src, dst_ref=dst, send_sem=ssem, recv_sem=rsem, device_id=to, device_id_type=MESH
         )
 
-    own_z = pltpu.make_async_copy(zc_ref.at[a], zin.at[a], zlocal)
-    own_z.start()
-    z_copies = []
-    for d in range(1, areas):
-        to = lax.rem(a + d, areas)
-        copy = send(zc_ref.at[to], zin.at[a], zs.at[d], zr.at[d], (to, r))
+    def mate(e):
+        return zi * inner + lax.rem(xi + e, inner)
+
+    def part_of(plane, p):
+        return zc_ref.at[:, pl.ds(pl.multiple_of((plane * pieces + p) * width, 128), width)]
+
+    z_sends = []
+    own_z = []
+    for p in range(pieces):
+        copy = pltpu.make_async_copy(part_of(zi, p), zin.at[p, a], zlocal.at[p])
         copy.start()
-        z_copies.append(copy)
+        own_z.append(copy)
+        for d in range(1, outer):
+            plane = lax.rem(zi + d, outer)
+            copy = send(part_of(plane, p), zin.at[p, a], zs.at[p, d], zr.at[p, a], (plane * inner + xi, r))
+            copy.start()
+            z_sends.append(copy)
+        for e in range(1, inner):
+            copy = send(part_of(zi, p), zin.at[p, a], zf.at[p, 0, e], zr.at[p, a], (mate(e), r))
+            copy.start()
+            z_sends.append(copy)
+
+    def relay_z(p):
+        for d in range(1, outer):
+            owner = lax.rem(zi + outer - d, outer) * inner + xi
+            block = zin.at[p, owner]
+            send(block, block, zs.at[p, d], zr.at[p, owner], (owner, r)).wait_recv()
+            for e in range(1, inner):
+                copy = send(block, block, zf.at[p, d, e], zr.at[p, owner], (mate(e), r))
+                copy.start()
+                z_sends.append(copy)
 
     index = columns(index_ref[...].astype(F32), probes).astype(jnp.int32)
     for c in range(nodes // 128):
@@ -198,7 +236,13 @@
         put_state(after)
         return carry
 
-    lax.fori_loop(0, STEPS, step, 0)
+    stops = [STEPS * 9 // 10 - (pieces - 1 - p) * STEPS * 2 // 5 for p in range(pieces)]
+    at = 0
+    for p, stop in enumerate(stops):
+        lax.fori_loop(at, stop, step, 0)
+        relay_z(p)
+        at = stop
+    lax.fori_loop(at, STEPS, step, 0)
     cin[a, r] = current_ref[...] * (2.0 / STEPS)
 
     copies = []
@@ -215,9 +259,6 @@
         copy = send(block, block, cs.at[d], cr.at[d], (lax.rem(a + d, areas), r))
         copy.start()
         copies.append(copy)
-    own_z.wait()
-    for copy in z_copies:
-        copy.wait()
     for copy in copies:
         copy.wait()
     members = group * ports
@@ -232,51 +273,139 @@
     high, low = split(flat_ref[...])
     rh[...] = high
     rl[...] = low
-    high, low = split(zin[...].reshape(areas * depth, chunk).T)
-    total = mm(high, rh[...]) + mm(low, rh[...]) + mm(high, rl[...])
-    mine[0] = total[:, 0:128]
-    mine[1] = total[:, 128:256]
-
-    inner = 2 ** ((areas.bit_length() - 1) // 2)
-    outer = areas // inner
-    zi = lax.div(a, inner)
-    xi = lax.rem(a, inner)
-
-    def region(part, who):
-        return bus_ref.at[part, pl.ds(pl.multiple_of(who * chunk, 8), chunk), :]
-
-    pending = []
-    arrivals = []
-    for part in range(2):
-        local = pltpu.make_async_copy(mine.at[part], region(part, a), olocal.at[part])
-        local.start()
-        pending.append(local)
-        for d in range(1, inner):
-            to = zi * inner + lax.rem(xi + d, inner)
-            k = part * areas + d
-            copy = send(mine.at[part], region(part, a), os.at[k], orr.at[k], (to, r))
-            copy.start()
-            pending.append(copy)
-        for d in range(1, outer):
-            to = lax.rem(zi + d, outer) * inner + xi
-            k = part * areas + inner * d
-            copy = send(mine.at[part], region(part, a), os.at[k], orr.at[k], (to, r))
-            copy.start()
-            arrivals.append((part, d, copy))
-    for part, d, copy in arrivals:
-        copy.wait_recv()
-        source = lax.rem(zi + outer - d, outer) * inner + xi
+
+    for p in range(pieces):
+        own_z[p].wait()
+    for copy in z_sends:
+        copy.wait_send()
+    for p in range(pieces):
         for e in range(1, inner):
-            to = zi * inner + lax.rem(xi + e, inner)
-            k = part * areas + inner * d + e
-            block = region(part, source)
-            forward = send(block, block, fs.at[k], fr.at[k], (to, r))
-            forward.start()
-            pending.append(forward)
-    for _, _, copy in arrivals:
-        copy.wait_send()
-    for copy in pending:
-        copy.wait()
+            for q in range(outer):
+                owner = q * inner + lax.rem(xi + e, inner)
+                block = zin.at[p, owner]
+                send(block, block, zf.at[p, 0, e], zr.at[p, owner], (owner, r)).wait_recv()
+
+    def product(p):
+        high, low = split(zin[p].reshape(areas * depth, width).T)
+        total = mm(high, rh[...]) + mm(low, rh[...]) + mm(high, rl[...])
+        keep = min(width, span_rows)
+        rows = pl.ds(pl.multiple_of(zi * span_rows + p * width, 8), keep)
+        vbus[0, rows, :] = total[:keep, 0:128]
+        vbus[1, rows, :] = total[:keep, 128:256]
+
+    cuts = SUBS
+    sub = chunk // cuts
+
+    def region(plane, x, k):
+        top = pl.multiple_of(plane * span_rows + x * chunk + k * sub, 8)
+        return vbus.at[:, pl.ds(top, sub), :]
+
+    def emit(plane, x, count, sem):
+        rows = pl.ds(pl.multiple_of(plane * span_rows + x * chunk, 8), count)
+        return pltpu.make_async_copy(vbus.at[:, rows, :], bus_ref.at[:, rows, :], sem)
+
+    def plane_at(plane):
+        return (plane * inner + xi, r)
+
+    can_up = zi + 1 < outer
+    can_down = zi >= 1
+
+    def launch(k):
+        up = send(region(zi, xi, k), region(zi, xi, k), os.at[0, k], orr.at[zi, k], plane_at(zi + 1))
+        down = send(region(zi, xi, k), region(zi, xi, k), os.at[1, k], orr.at[zi, k], plane_at(zi - 1))
+        return up, down
+
+    if pieces == inner:
+        product(xi)
+    else:
+        for p in range(pieces):
+            product(p)
+    for k in range(cuts):
+        up, down = launch(k)
+        pl.when(can_up)(up.start)
+        pl.when(can_down)(down.start)
+    if pieces == inner:
+        for i in range(1, pieces):
+            product(lax.rem(xi + i, inner))
+    local = emit(zi, 0, span_rows, olocal.at[0, 0, 0])
+    local.start()
+
+    def hops(d):
+        return ((zi - d, zi - d >= 0, zi + 1, can_up), (zi + d, zi + d < outer, zi - 1, can_down))
+
+    def relay(plane, k, d, side, ahead):
+        block = region(plane, xi, k)
+        onward = send(block, block, fs.at[side, d, k], orr.at[plane, k], plane_at(ahead))
+        across = [
+            send(block, block, xf.at[side, d, e, k], xr.at[plane, xi, k], (mate(e), r)) for e in range(1, inner)
+        ]
+        return onward, across
+
+    for d in range(1, outer):
+        for k in range(cuts):
+            for side, (plane, have, ahead, go) in enumerate(hops(d)):
+
+                @pl.when(have)
+                def _(plane=plane, k=k, d=d, side=side, ahead=ahead, go=go):
+                    onward, across = relay(plane, k, d, side, ahead)
+                    onward.wait_recv()
+                    pl.when(go)(onward.start)
+                    for copy in across:
+                        copy.start()
+
+    for d in range(1, outer):
+        for side, (plane, have, ahead, go) in enumerate(hops(d)):
+
+            @pl.when(have)
+            def _(plane=plane, d=d, side=side):
+                emit(plane, xi, chunk, olocal.at[side, d, 0]).start()
+                for e in range(1, inner):
+                    x = lax.rem(xi + e, inner)
+                    for k in range(cuts):
+                        block = region(plane, x, k)
+                        send(block, block, xf.at[side, d, e, k], xr.at[plane, x, k], (mate(e), r)).wait_recv()
+                    emit(plane, x, chunk, olocal.at[side, d, e]).start()
+
+    members = port_bus_ref.shape[0] // group
+    for j in range(group):
+        for p in range(members):
+            place = port_bus_ref[j * members + p] - r * bus_ref.shape[1]
+            inside = (place >= 0) & (place < bus_ref.shape[1])
+            place = jnp.clip(place, 0, bus_ref.shape[1] - 1)
+            for part in range(2):
+                value = vbus[part, pl.ds(place, 1), :]
+                picked[j, part, p : p + 1, :] = jnp.where(inside, value, 0.0)
+
+    def hand(d):
+        to = lax.rem(r + d, group)
+        return send(picked.at[to], landed.at[r], ps.at[d], pr.at[d], (a, to))
+
+    for d in range(1, group):
+        hand(d).start()
+    for d in range(1, outer):
+        for side, (plane, have, ahead, go) in enumerate(hops(d)):
+
+            @pl.when(have)
+            def _(plane=plane, d=d, side=side, ahead=ahead, go=go):
+                for k in range(cuts):
+                    onward, across = relay(plane, k, d, side, ahead)
+                    pl.when(go)(onward.wait_send)
+                    for copy in across:
+                        copy.wait_send()
+                for e in range(inner):
+                    emit(plane, lax.rem(xi + e, inner), chunk, olocal.at[side, d, e]).wait()
+
+    for k in range(cuts):
+        up, down = launch(k)
+        pl.when(can_up)(up.wait_send)
+        pl.when(can_down)(down.wait_send)
+    for d in range(1, group):
+        hand(d).wait()
+    value = picked[r]
+    for d in range(1, group):
+        value = value + landed[lax.rem(r + d, group)]
+    port_ref[...] = value
+    local.wait()
 
 
 def vmem():
@@ -328,9 +457,13 @@
     group = lax.axis_size("row")
     bus_rows = transfer_impedance.shape[1]
     members = transfer_impedance.shape[2]
-    chunk = bus_rows // areas
-    zt = jnp.transpose(transfer_impedance, (0, 2, 1)).reshape(2 * members, bus_rows)
-    zc = jnp.transpose(zt.reshape(2 * members, areas, chunk), (1, 0, 2))
+    inner = 2 ** ((areas.bit_length() - 1) // 2)
+    outer = areas // inner
+    span_rows = bus_rows // outer
+    padded = -(-span_rows // 128) * 128
+    pieces = 2 if padded % 256 == 0 else 1
+    zc = jnp.transpose(transfer_impedance, (0, 2, 1)).reshape(2 * members, outer, span_rows)
+    zc = jnp.pad(zc, ((0, 0), (0, 0), (0, padded - span_rows))).reshape(2 * members, outer * padded)
 
     pad = 128 - lines - convs - ports
     index = jnp.concatenate([line_node, conv_node, port_node, jnp.full((1, pad), -1, jnp.int32)], axis=1)
@@ -346,16 +479,16 @@
     angles = jnp.arange(1, STEPS + 1, dtype=F32) * jnp.float32(2.0 * math.pi / STEPS)
     trig = jnp.stack([jnp.cos(angles), jnp.sin(angles)])
     flops = 2 * STEPS * (nodes + 128) * (2 * nodes + 256) * 256
-    waves, hist_end, conv_out, _, bus_voltage = pl.pallas_call(
+    waves, hist_end, conv_out, port_voltage, bus_voltage = pl.pallas_call(
         functools.partial(window_kernel, lines, convs, ports),
         out_shape=(
             jax.ShapeDtypeStruct((STEPS, lines, cases), F32),
             jax.ShapeDtypeStruct((nodes, cases), F32),
             jax.ShapeDtypeStruct((2, convs, cases), F32),
-            jax.ShapeDtypeStruct((areas * 2 * members, 2 * cases), F32),
+            jax.ShapeDtypeStruct((2, ports, cases), F32),
             jax.ShapeDtypeStruct((2, bus_rows, cases), F32),
         ),
-        in_specs=[smem()] * 4 + [vmem()] * 12 + [pl.BlockSpec(memory_space=pl.ANY)],
+        in_specs=[smem()] * 4 + [vmem()] * 12 + [smem(), pl.BlockSpec(memory_space=pl.ANY)],
         out_specs=(vmem(),) * 4 + (pl.BlockSpec(memory_space=pl.ANY),),
         scratch_shapes=[
             pltpu.VMEM((nodes + 128, 2 * nodes + 256), BF16),
@@ -364,23 +497,30 @@
             pltpu.VMEM((128, nodes), F32),
             pltpu.VMEM((128, 128), F32),
             pltpu.VMEM((2, ports, cases), F32),
-            pltpu.VMEM((areas, 2 * members, chunk), F32),
+            pltpu.VMEM((pieces, areas, 2 * members, padded // pieces), F32),
             pltpu.VMEM((areas, group, 2, ports, cases), F32),
-            pltpu.VMEM((2, chunk, cases), F32),
+            pltpu.VMEM((2, bus_rows, cases), F32),
+            pltpu.VMEM((areas * 2 * members, 2 * cases), F32),
             pltpu.VMEM((areas * 2 * members, 2 * cases), BF16),
             pltpu.VMEM((areas * 2 * members, 2 * cases), BF16),
-            pltpu.SemaphoreType.DMA((areas,)),
-            pltpu.SemaphoreType.DMA((areas,)),
+            pltpu.SemaphoreType.DMA((pieces, outer)),
+            pltpu.SemaphoreType.DMA((pieces, areas)),
+            pltpu.SemaphoreType.DMA((pieces, outer, inner)),
             pltpu.SemaphoreType.DMA((group,)),
             pltpu.SemaphoreType.DMA((group,)),
             pltpu.SemaphoreType.DMA((areas,)),
             pltpu.SemaphoreType.DMA((areas,)),
-            pltpu.SemaphoreType.DMA,
-            pltpu.SemaphoreType.DMA((2 * areas,)),
-            pltpu.SemaphoreType.DMA((2 * areas,)),
-            pltpu.SemaphoreType.DMA((2 * areas,)),
-            pltpu.SemaphoreType.DMA((2 * areas,)),
-            pltpu.SemaphoreType.DMA((2,)),
+            pltpu.SemaphoreType.DMA((pieces,)),
+            pltpu.SemaphoreType.DMA((2, SUBS)),
+            pltpu.SemaphoreType.DMA((outer, SUBS)),
+            pltpu.SemaphoreType.DMA((2, outer, SUBS)),
+            pltpu.SemaphoreType.DMA((2, outer, inner, SUBS)),
+            pltpu.SemaphoreType.DMA((outer, inner, SUBS)),
+            pltpu.SemaphoreType.DMA((2, outer, inner)),
+            pltpu.VMEM((group, 2, ports, cases), F32),
+            pltpu.VMEM((group, 2, ports, cases), F32),
+            pltpu.SemaphoreType.DMA((group,)),
+            pltpu.SemaphoreType.DMA((group,)),
         ],
         compiler_params=pltpu.CompilerParams(collective_id=0, has_side_effects=True),
         cost_estimate=pl.CostEstimate(flops=flops, bytes_accessed=8_000_000, transcendentals=0),
@@ -402,18 +542,11 @@
         conv_state[0],
         conv_reference[0],
         port_voltage_prev[:, 0],
+        port_bus.reshape(-1),
         zc,
     )
 
-    local = port_bus.reshape(-1) - lax.axis_index("row") * bus_rows
-    inside = (local >= 0) & (local < bus_rows)
-    local = jnp.clip(local, 0, bus_rows - 1)
-    chosen = jnp.concatenate([local, local + bus_rows])
-    taken = jnp.take(bus_voltage.reshape(2 * bus_rows, cases), chosen, axis=0, mode="clip")
-    taken = jnp.where(jnp.concatenate([inside, inside])[:, None], taken, 0.0)
-    taken = taken.reshape(2, port_bus.shape[0], port_bus.shape[1], cases)
-    port_voltage = lax.psum_scatter(taken, "row", scatter_dimension=1, tiled=True)
-    return (waves[None], hist_end[None], conv_out[None], bus_voltage, port_voltage)
+    return (waves[None], hist_end[None], conv_out[None], bus_voltage, port_voltage[:, None])
 
 
 def solution(mesh):

time: 181 us -> 150 us (0.83)
  the two profiles are of different devices: /device:TPU:16 before, /device:TPU:0 now
where the time goes in v1:
time: 150 us
  Pallas kernels  112 us (75%)
  local copies, waits for them, and re-layouts  14.1 us (9%)
  waiting for transfers between devices  8.98 us (6%)
  starting transfers between devices  8.2 us (5%)
  other arithmetic  5.14 us (3%)
    pallas_call x1, Pallas kernels, per_device(): pl.pallas_call(functools.partial(window_kernel, lines, convs, ports), out...  112 us
    unnamed x15, local copies, waits for them, and re-layouts  11.6 us
    ppermute x4, waiting for transfers between devices, shifted(): return lax.ppermute(x, axes, [(i, (i + by) % size) for i in range(size)])  8.98 us
    ppermute x4, starting transfers between devices, shifted(): return lax.ppermute(x, axes, [(i, (i + by) % size) for i in range(size)])  8.2 us
  transfers between devices with their start and end apart: 4, of which 3 were waited for; matrix products, arithmetic and copies ran while one was open for 4% of the time, Pallas kernels for 0%

profile of v1, /device:TPU:0, one launch (start us, length us, event | category | flops | bytes accessed | tf_op | source)
XLA Modules:
  0.0 149.8 jit_solution(13572209163694432689)
XLA Ops:
  0.6 1.1 fusion.3
  1.8 7.0 %collective-permute-start.3 = (f32[40,16,128]{2,1,0:T(8,128)S(1)}, f32[40,16,128]{2,1,0:T(8,128)S(1)}, u32[]{:S(2)}, u32[]{:S(2)}) collective-permute-start(f32[40,16,128]{2,1,0:T(8,128)S(1)} %get-tuple-element.20), channel_id=1, source_target_pairs={{0,30},{1,31},{2,0},{3,1},{4,2},{5,3},{6,4},{7,5},{8,6},{9,7},{10,... | collective-permute-start | bytes 983048 | tf_op jit(solution)/shard_map/ppermute | solution.py:23
  8.8 0.0 collective-permute-start.2
  8.8 1.2 collective-permute-start.1
  10.0 0.0 collective-permute-start
  10.7 0.7 broadcast_multiply_fusion
  11.3 1.4 reshape.37.port_bus_ref
  12.7 0.6 pad_maximum_fusion.trig_ref
  13.3 1.3 maximum_maximum_fusion.coef_ref
  14.6 1.3 bitcast_add_fusion.index_ref
  15.9 1.2 and_select_fusion.reach_ref
  17.1 0.0 collective-permute-done.3.above2_ref
  17.1 0.0 copy-start.1
  17.1 2.1 %collective-permute-done.2.above1_ref = f32[40,16,128]{2,1,0:T(8,128)S(1)} collective-permute-done((f32[40,16,128]{2,1,0:T(8,128)S(1)}, f32[40,16,128]{2,1,0:T(8,128)S(1)}, u32[]{:S(2)}, u32[]{:S(2)}) %collective-permute-start.2) | collective-permute-done | bytes 327712 | tf_op jit(solution)/shard_map/ppermute | solution.py:23
  19.3 0.0 copy-start.2
  19.3 4.0 %collective-permute-done.1.below2_ref = f32[40,16,128]{2,1,0:T(8,128)S(1)} collective-permute-done((f32[40,16,128]{2,1,0:T(8,128)S(1)}, f32[40,16,128]{2,1,0:T(8,128)S(1)}, u32[]{:S(2)}, u32[]{:S(2)}) %collective-permute-start.1) | collective-permute-done | bytes 327712 | tf_op jit(solution)/shard_map/ppermute | solution.py:23
  23.3 0.0 copy-start.3
  23.3 2.8 %collective-permute-done.below1_ref = f32[40,16,128]{2,1,0:T(8,128)S(1)} collective-permute-done((f32[40,16,128]{2,1,0:T(8,128)S(1)}, f32[40,16,128]{2,1,0:T(8,128)S(1)}, u32[]{:S(2)}, u32[]{:S(2)}) %collective-permute-start) | collective-permute-done | bytes 327712 | tf_op jit(solution)/shard_map/ppermute | solution.py:23
  26.1 0.0 copy-start.4
  26.1 0.0 copy-done.1
  26.1 0.0 copy-done.2
  26.1 0.0 copy-done.3
  26.1 0.7 copy-done.4
  26.8 112.1 %window.1 = (f32[20,32,128]{2,1,0:T(8,128)}, f32[1024,128]{1,0:T(8,128)}, f32[2,64,128]{2,1,0:T(8,128)}, f32[2,8,128]{2,1,0:T(8,128)}, f32[2,5120,128]{2,1,0:T(8,128)}) custom-call(s32[32]{0:T(128)} %and_select_fusion.reach_ref, s32[32]{0:T(128)} %bitcast.31, f32[2,20]{1,0:T(2,128)} %pad_maximum_fusion.trig_ref, s32[1]{0:T(128)S(6)} %copy.30.count_ref, ...), custom_call_target="tpu_custom_call" | custom-call | flops 27179089920 | bytes 8000000 | tf_op jit(solution)/shard_map/window/pallas_call | solution.py:482
  138.9 1.7 %copy.31 = f32[1,20,32,128]{3,2,1,0:T(8,128)} copy(f32[1,20,32,128]{3,2,1,0:T(8,128)} %bitcast.22) | data formatting | bytes 655360
  140.6 1.9 %copy.32 = f32[1,1024,128]{2,1,0:T(8,128)} copy(f32[1,1024,128]{2,1,0:T(8,128)} %bitcast.21) | data formatting | bytes 1048576
  142.5 1.5 copy.33
  144.0 0.0 copy-start
  144.0 5.2 %copy.34 = f32[2,5120,128]{2,1,0:T(8,128)} copy(f32[2,5120,128]{2,1,0:T(8,128)} %get-tuple-element.32) | data formatting | bytes 10485760
  149.2 0.0 copy-done
  149.2 0.6 copy.35
  (5 shorter events, 0.1 us)
Async XLA Ops:
  1.8 15.4 %collective-permute-start.3 = (f32[40,16,128]{2,1,0:T(8,128)S(1)}, f32[40,16,128]{2,1,0:T(8,128)S(1)}, u32[]{:S(2)}, u32[]{:S(2)}) collective-permute-start(f32[40,16,128]{2,1,0:T(8,128)S(1)} %get-tuple-element.20), channel_id=1, source_target_pairs={{0,30},{1,31},{2,0},{3,1},{4,2},{5,3},{6,4},{7,5},{8,6},{9,7},{10,... | collective-permute-start | bytes 983048 | tf_op jit(solution)/shard_map/ppermute | solution.py:23
  8.8 10.5 %collective-permute-start.2 = (f32[40,16,128]{2,1,0:T(8,128)S(1)}, f32[40,16,128]{2,1,0:T(8,128)S(1)}, u32[]{:S(2)}, u32[]{:S(2)}) collective-permute-start(f32[40,16,128]{2,1,0:T(8,128)S(1)} %get-tuple-element.20), channel_id=1, source_target_pairs={{0,31},{1,0},{2,1},{3,2},{4,3},{5,4},{6,5},{7,6},{8,7},{9,8},{10,9... | collective-permute-start | bytes 983048 | tf_op jit(solution)/shard_map/ppermute | solution.py:23
  8.8 14.5 %collective-permute-start.1 = (f32[40,16,128]{2,1,0:T(8,128)S(1)}, f32[40,16,128]{2,1,0:T(8,128)S(1)}, u32[]{:S(2)}, u32[]{:S(2)}) collective-permute-start(f32[40,16,128]{2,1,0:T(8,128)S(1)} %get-tuple-element.21), channel_id=1, source_target_pairs={{0,2},{1,3},{2,4},{3,5},{4,6},{5,7},{6,8},{7,9},{8,10},{9,11},{10,... | collective-permute-start | bytes 983048 | tf_op jit(solution)/shard_map/ppermute | solution.py:23
  10.0 16.1 %collective-permute-start = (f32[40,16,128]{2,1,0:T(8,128)S(1)}, f32[40,16,128]{2,1,0:T(8,128)S(1)}, u32[]{:S(2)}, u32[]{:S(2)}) collective-permute-start(f32[40,16,128]{2,1,0:T(8,128)S(1)} %get-tuple-element.21), channel_id=1, source_target_pairs={{0,1},{1,2},{2,3},{3,4},{4,5},{5,6},{6,7},{7,8},{8,9},{9,10},{10,1... | collective-permute-start | bytes 983048 | tf_op jit(solution)/shard_map/ppermute | solution.py:23
  17.1 9.0 %copy-start.1 = (f32[40,16,128]{2,1,0:T(8,128)}, f32[40,16,128]{2,1,0:T(8,128)S(1)}, u32[]{:S(2)}) copy-start(f32[40,16,128]{2,1,0:T(8,128)S(1)} %collective-permute-done.3.above2_ref) | copy-start | bytes 983044
  19.3 6.9 %copy-start.2 = (f32[40,16,128]{2,1,0:T(8,128)}, f32[40,16,128]{2,1,0:T(8,128)S(1)}, u32[]{:S(2)}) copy-start(f32[40,16,128]{2,1,0:T(8,128)S(1)} %collective-permute-done.2.above1_ref) | copy-start | bytes 983044
  23.3 2.8 %copy-start.3 = (f32[40,16,128]{2,1,0:T(8,128)}, f32[40,16,128]{2,1,0:T(8,128)S(1)}, u32[]{:S(2)}) copy-start(f32[40,16,128]{2,1,0:T(8,128)S(1)} %collective-permute-done.1.below2_ref) | copy-start | bytes 983044
  26.1 0.7 copy-start.4
  144.0 5.2 %copy-start = (f32[2,8,128]{2,1,0:T(8,128)S(1)}, f32[2,8,128]{2,1,0:T(8,128)}, u32[]{:S(2)}) copy-start(f32[2,8,128]{2,1,0:T(8,128)} %get-tuple-element.14) | copy-start | bytes 24580

commit v2 on v1

--- a/solution.py
+++ b/solution.py
@@ -3,24 +3,19 @@
 
 import jax
 import jax.numpy as jnp
+import numpy as np
 from jax import lax
 from jax.experimental import pallas as pl
 from jax.experimental.pallas import tpu as pltpu
 from jax.sharding import PartitionSpec as P
 
 STEPS = 20
-HIST = 40
 SAG_FACTOR = 0.3
 F32 = jnp.float32
 BF16 = jnp.bfloat16
 MESH = pl.DeviceIdType.MESH
 SUBS = 10
-
-
-def shifted(x, by):
-    axes = ("area", "row")
-    size = lax.axis_size(axes)
-    return lax.ppermute(x, axes, [(i, (i + by) % size) for i in range(size)])
+NEAR = 12
 
 
 def split(x):
@@ -40,19 +35,21 @@
     lines,
     convs,
     ports,
-    reach_ref,
+    partner_ref,
     delay_ref,
     trig_ref,
     count_ref,
-    index_ref,
-    coef_ref,
+    line_node_ref,
+    conv_node_ref,
+    port_node_ref,
+    line_adm_ref,
+    conv_rate_ref,
+    conv_limit_ref,
+    port_adm_ref,
     ginv_ref,
     gcap_ref,
     hist_ref,
-    below1_ref,
-    below2_ref,
-    above1_ref,
-    above2_ref,
+    past_ref,
     state_ref,
     target_ref,
     pvolt_ref,
@@ -93,6 +90,11 @@
     landed,
     ps,
     pr,
+    sorted_out,
+    sorted_in,
+    base_ref,
+    ws,
+    wr,
 ):
     nodes = ginv_ref.shape[0]
     probes = 128
@@ -109,17 +111,55 @@
     zi = lax.div(a, inner)
     xi = lax.rem(a, inner)
 
+    def subnet(by):
+        to = lax.rem(a * group + r + by + areas * group, areas * group)
+        return (lax.div(to, group), lax.rem(to, group))
+
     barrier = pltpu.get_barrier_semaphore()
     for d in range(1, areas):
         pl.semaphore_signal(barrier, inc=1, device_id=(lax.rem(a + d, areas), r), device_id_type=MESH)
     for d in range(1, group):
         pl.semaphore_signal(barrier, inc=1, device_id=(a, lax.rem(r + d, group)), device_id_type=MESH)
-    pl.semaphore_wait(barrier, areas + group - 2)
+    for by in (1, -1, 2, -2):
+        pl.semaphore_signal(barrier, inc=1, device_id=subnet(by), device_id_type=MESH)
+
+    hist_steps = past_ref.shape[0] // lines
+    near = []
+    place = []
+    seen = jnp.int32(0)
+    for l in range(half):
+        gap = partner_ref[l] - (a * group + r)
+        near.append((gap == 1) | (gap == 1 - areas * group))
+        place.append(jnp.where(near[l], seen, NEAR + l - seen))
+        seen = seen + jnp.where(near[l], 1, 0)
+    for l in range(lines):
+        start = jnp.clip(hist_steps - delay_ref[l], 0, hist_steps - STEPS)
+        base_ref[l] = jnp.clip(place[l % half], 0, half - 1) * hist_steps + start
+    for k in range(half):
+        line = jnp.int32(0)
+        for l in range(half):
+            line = line + jnp.where(place[l] == k, l, 0)
+        line = jnp.clip(line, 0, half - 1)
+        slot = pl.ds(k * hist_steps, hist_steps)
+        sorted_out[0, slot, :] = past_ref[pl.ds(line, hist_steps, stride=lines), :]
+        sorted_out[1, slot, :] = past_ref[pl.ds(line + half, hist_steps, stride=lines), :]
+    pl.semaphore_wait(barrier, areas + group + 2)
 
     def send(src, dst, ssem, rsem, to):
         return pltpu.make_async_remote_copy(
             src_ref=src, dst_ref=dst, send_sem=ssem, recv_sem=rsem, device_id=to, device_id_type=MESH
         )
+
+    wave_sends = []
+    edge = NEAR * hist_steps
+    for side, way in enumerate((1, -1)):
+        for reach, slots in ((1, pl.ds(0, edge)), (2, pl.ds(edge, half * hist_steps - edge))):
+            sem = 2 * side + reach - 1
+            copy = send(
+                sorted_out.at[side, slots, :], sorted_in.at[side, slots, :], ws.at[sem], wr.at[sem], subnet(way * reach)
+            )
+            copy.start()
+            wave_sends.append(copy)
 
     def mate(e):
         return zi * inner + lax.rem(xi + e, inner)
@@ -153,7 +193,16 @@
                 copy.start()
                 z_sends.append(copy)
 
-    index = columns(index_ref[...].astype(F32), probes).astype(jnp.int32)
+    pad = probes - lines - convs - ports
+
+    def stacked(line, conv, port, rest):
+        return jnp.concatenate(
+            [columns(line, lines), columns(conv, convs), columns(port, ports), jnp.full((pad, 128), rest, F32)], axis=0
+        )
+
+    index = stacked(
+        line_node_ref[...].astype(F32), conv_node_ref[...].astype(F32), port_node_ref[...].astype(F32), -1.0
+    ).astype(jnp.int32)
     for c in range(nodes // 128):
         lane = lax.broadcasted_iota(jnp.int32, (probes, 128), 1) + 128 * c
         cap2[:, c * 128 : (c + 1) * 128] = jnp.where(index == lane, 1.0, 0.0)
@@ -180,11 +229,10 @@
     put_state(hist_ref[...])
     state_out_ref[...] = state_ref[...]
     current_ref[...] = jnp.zeros_like(current_ref)
-    coef = coef_ref[...]
-    two_adm = columns(coef[0:1], 128)[0:lines]
-    rate = columns(coef[1:2], 128)[lines : lines + convs]
-    limit = columns(coef[2:3], 128)[lines : lines + convs]
-    padm = columns(coef[0:1], 128)[lines + convs : lines + convs + ports]
+    two_adm = 2.0 * columns(line_adm_ref[...], lines)
+    rate = columns(conv_rate_ref[...], convs)
+    limit = columns(conv_limit_ref[...], convs)
+    padm = columns(port_adm_ref[...], ports)
     live = lax.broadcasted_iota(jnp.int32, (convs, 128), 0) < count_ref[0]
     xs[lines + convs + ports :, :] = jnp.zeros((probes - lines - convs - ports, 128), F32)
 
@@ -192,13 +240,8 @@
         cosine = trig_ref[0, t]
         sine = trig_ref[1, t]
         for l in range(half):
-            up = jnp.clip(t - delay_ref[l] + HIST, 0, HIST - 1)
-            down = jnp.clip(t - delay_ref[l + half] + HIST, 0, HIST - 1)
-            near = reach_ref[l] == 1
-            xs[l : l + 1, :] = jnp.where(near, above1_ref[up, l : l + 1, :], above2_ref[up, l : l + 1, :])
-            xs[l + half : l + half + 1, :] = jnp.where(
-                near, below1_ref[down, l : l + 1, :], below2_ref[down, l : l + 1, :]
-            )
+            xs[l : l + 1, :] = sorted_in[1, pl.ds(base_ref[l] + t, 1), :]
+            xs[l + half : l + half + 1, :] = sorted_in[0, pl.ds(base_ref[l + half] + t, 1), :]
         inward = xs[0:lines, :]
         axial = state_out_ref[0]
         normal = state_out_ref[1]
@@ -235,6 +278,9 @@
         hist_out_ref[...] = after
         put_state(after)
         return carry
+
+    for copy in wave_sends:
+        copy.wait()
 
     stops = [STEPS * 9 // 10 - (pieces - 1 - p) * STEPS * 2 // 5 for p in range(pieces)]
     at = 0
@@ -437,22 +483,10 @@
     port_bus,
     transfer_impedance,
 ):
-    subnets = lax.axis_size(("area", "row"))
-    own = lax.axis_index(("area", "row"))
-    history = wave_history[0]
-    lines = history.shape[1]
-    half = lines // 2
-    cases = history.shape[2]
+    steps_kept, lines, cases = wave_history.shape[1:]
     nodes = conductance_inverse.shape[1]
     convs = conv_node.shape[1]
     ports = port_node.shape[1]
-    upper = history[:, :half]
-    lower = history[:, half:]
-    below1 = shifted(upper, 1)
-    above1 = shifted(lower, -1)
-    below2 = shifted(upper, 2)
-    above2 = shifted(lower, -2)
-    reach = (line_partner[0] - own) % subnets
     areas = lax.axis_size("area")
     group = lax.axis_size("row")
     bus_rows = transfer_impedance.shape[1]
@@ -465,19 +499,8 @@
     zc = jnp.transpose(transfer_impedance, (0, 2, 1)).reshape(2 * members, outer, span_rows)
     zc = jnp.pad(zc, ((0, 0), (0, 0), (0, padded - span_rows))).reshape(2 * members, outer * padded)
 
-    pad = 128 - lines - convs - ports
-    index = jnp.concatenate([line_node, conv_node, port_node, jnp.full((1, pad), -1, jnp.int32)], axis=1)
-    ones = jnp.ones((1, 128 - lines - convs), F32)
-    coef = jnp.concatenate(
-        [
-            jnp.concatenate([2.0 * line_admittance, jnp.ones((1, convs), F32), port_admittance, ones[:, :pad]], axis=1),
-            jnp.concatenate([jnp.ones((1, lines), F32), conv_rate, ones], axis=1),
-            jnp.concatenate([jnp.ones((1, lines), F32), conv_limit, ones], axis=1),
-        ],
-        axis=0,
-    )
-    angles = jnp.arange(1, STEPS + 1, dtype=F32) * jnp.float32(2.0 * math.pi / STEPS)
-    trig = jnp.stack([jnp.cos(angles), jnp.sin(angles)])
+    angles = np.arange(1, STEPS + 1, dtype=np.float32) * np.float32(2.0 * math.pi / STEPS)
+    trig = jnp.asarray(np.stack([np.cos(angles), np.sin(angles)]).astype(np.float32))
     flops = 2 * STEPS * (nodes + 128) * (2 * nodes + 256) * 256
     waves, hist_end, conv_out, port_voltage, bus_voltage = pl.pallas_call(
         functools.partial(window_kernel, lines, convs, ports),
@@ -488,7 +511,7 @@
             jax.ShapeDtypeStruct((2, ports, cases), F32),
             jax.ShapeDtypeStruct((2, bus_rows, cases), F32),
         ),
-        in_specs=[smem()] * 4 + [vmem()] * 12 + [smem(), pl.BlockSpec(memory_space=pl.ANY)],
+        in_specs=[smem()] * 4 + [vmem()] * 14 + [smem(), pl.BlockSpec(memory_space=pl.ANY)],
         out_specs=(vmem(),) * 4 + (pl.BlockSpec(memory_space=pl.ANY),),
         scratch_shapes=[
             pltpu.VMEM((nodes + 128, 2 * nodes + 256), BF16),
@@ -521,24 +544,31 @@
             pltpu.VMEM((group, 2, ports, cases), F32),
             pltpu.SemaphoreType.DMA((group,)),
             pltpu.SemaphoreType.DMA((group,)),
+            pltpu.VMEM((2, lines // 2 * steps_kept, cases), F32),
+            pltpu.VMEM((2, lines // 2 * steps_kept, cases), F32),
+            pltpu.SMEM((lines,), jnp.int32),
+            pltpu.SemaphoreType.DMA((4,)),
+            pltpu.SemaphoreType.DMA((4,)),
         ],
         compiler_params=pltpu.CompilerParams(collective_id=0, has_side_effects=True),
         cost_estimate=pl.CostEstimate(flops=flops, bytes_accessed=8_000_000, transcendentals=0),
         name="window",
     )(
-        reach,
+        line_partner[0],
         line_delay[0],
         trig,
         conv_count,
-        index,
-        coef,
+        line_node,
+        conv_node,
+        port_node,
+        line_admittance,
+        conv_rate,
+        conv_limit,
+        port_admittance,
         conductance_inverse[0],
         cap_conductance,
         cap_history[0],
-        below1,
-        below2,
-        above1,
-        above2,
+        wave_history.reshape(steps_kept * lines, cases),
         conv_state[0],
         conv_reference[0],
         port_voltage_prev[:, 0],

time: 150 us -> 136 us (0.907)
  Pallas kernels: 112 us -> 122 us
  waiting for transfers between devices: 8.98 us -> 0 us
  starting transfers between devices: 8.2 us -> 0 us
  other arithmetic: 5.14 us -> 0 us
  local copies, waits for them, and re-layouts: 14.1 us -> 12.1 us
    pallas_call x1, Pallas kernels: 112 us -> 122 us  [per_device(): pl.pallas_call(functools.partial(window_kernel, lines, convs, ports), out...]
    ppermute x4 -> x0, waiting for transfers between devices: 8.98 us -> none  [shifted(): return lax.ppermute(x, axes, [(i, (i + by) % size) for i in range(size)])]
    ppermute x4 -> x0, starting transfers between devices: 8.2 us -> none  [shifted(): return lax.ppermute(x, axes, [(i, (i + by) % size) for i in range(size)])]
    concatenate x2 -> x0, other arithmetic: 2.67 us -> none  [the longest x1 1.35 us: per_device(): jnp.concatenate([jnp.concatenate([2.0 * line_admittance, jnp.ones((1, con...]
    unnamed x15 -> x7, local copies, waits for them, and re-layouts: 11.6 us -> 10.9 us
  transfers between devices with their start and end apart: 4 -> 0, of which waited for: 3 -> 0; matrix products, arithmetic and copies ran while one was open for 4% -> 0% of each run, Pallas kernels for 0% -> 0%
where the time goes in v2:
time: 136 us
  Pallas kernels  122 us (90%)
  local copies, waits for them, and re-layouts  12.1 us (9%)
    pallas_call x1, Pallas kernels, per_device(): pl.pallas_call(functools.partial(window_kernel, lines, convs, ports), out...  122 us
    unnamed x7, local copies, waits for them, and re-layouts  10.9 us

profile of v2, /device:TPU:0, one launch (start us, length us, event | category | flops | bytes accessed | tf_op | source)
XLA Modules:
  0.0 135.8 jit_solution(2033068301153053766)
XLA Ops:
  1.3 1.3 reshape.22.port_bus_ref
  2.6 122.4 %window.1 = (f32[20,32,128]{2,1,0:T(8,128)}, f32[1024,128]{1,0:T(8,128)}, f32[2,64,128]{2,1,0:T(8,128)}, f32[2,8,128]{2,1,0:T(8,128)}, f32[2,5120,128]{2,1,0:T(8,128)}) custom-call(s32[32]{0:T(128)} %bitcast.28, s32[32]{0:T(128)} %bitcast.29, f32[2,20]{1,0:T(2,128)} %constant.1.clone.trig_ref, s32[1]{0:T(128)S(6)} %copy.31.count_ref, s32[1,32]{1,0:T(1,128)} %line_node_ref.1, ...), custom_call_target="tpu_custom_call" | custom-call | flops 27179089920 | bytes 8000000 | tf_op jit(solution)/shard_map/window/pallas_call | solution.py:505
  124.9 1.7 %copy.32 = f32[1,20,32,128]{3,2,1,0:T(8,128)} copy(f32[1,20,32,128]{3,2,1,0:T(8,128)} %bitcast.18) | data formatting | bytes 655360
  126.7 1.9 %copy.33 = f32[1,1024,128]{2,1,0:T(8,128)} copy(f32[1,1024,128]{2,1,0:T(8,128)} %bitcast.17) | data formatting | bytes 1048576
  128.5 1.5 %copy.34 = f32[1,2,64,128]{3,2,1,0:T(8,128)} copy(f32[1,2,64,128]{3,2,1,0:T(8,128)} %bitcast.19) | data formatting | bytes 131072
  130.0 0.0 copy-start
  130.0 5.2 %copy.35 = f32[2,5120,128]{2,1,0:T(8,128)} copy(f32[2,5120,128]{2,1,0:T(8,128)} %get-tuple-element.28) | data formatting | bytes 10485760
  135.2 0.0 copy-done
  135.2 0.6 copy.36
Async XLA Ops:
  130.0 5.2 %copy-start = (f32[2,8,128]{2,1,0:T(8,128)S(1)}, f32[2,8,128]{2,1,0:T(8,128)}, u32[]{:S(2)}) copy-start(f32[2,8,128]{2,1,0:T(8,128)} %get-tuple-element.14) | copy-start | bytes 24580

commit v3 on v2

--- a/solution.py
+++ b/solution.py
@@ -16,6 +16,7 @@
 MESH = pl.DeviceIdType.MESH
 SUBS = 10
 NEAR = 12
+EARLY = 24
 
 
 def split(x):
@@ -90,8 +91,10 @@
     landed,
     ps,
     pr,
-    sorted_out,
-    sorted_in,
+    out_early,
+    out_late,
+    in_early,
+    in_late,
     base_ref,
     ws,
     wr,
@@ -124,6 +127,8 @@
         pl.semaphore_signal(barrier, inc=1, device_id=subnet(by), device_id_type=MESH)
 
     hist_steps = past_ref.shape[0] // lines
+    late = hist_steps - EARLY
+    pieces_of = (((out_early, in_early), 0, EARLY), ((out_late, in_late), EARLY, late))
     near = []
     place = []
     seen = jnp.int32(0)
@@ -134,15 +139,17 @@
         seen = seen + jnp.where(near[l], 1, 0)
     for l in range(lines):
         start = jnp.clip(hist_steps - delay_ref[l], 0, hist_steps - STEPS)
-        base_ref[l] = jnp.clip(place[l % half], 0, half - 1) * hist_steps + start
+        base_ref[0, l] = jnp.clip(place[l % half], 0, half - 1)
+        base_ref[1, l] = start
     for k in range(half):
         line = jnp.int32(0)
         for l in range(half):
             line = line + jnp.where(place[l] == k, l, 0)
         line = jnp.clip(line, 0, half - 1)
-        slot = pl.ds(k * hist_steps, hist_steps)
-        sorted_out[0, slot, :] = past_ref[pl.ds(line, hist_steps, stride=lines), :]
-        sorted_out[1, slot, :] = past_ref[pl.ds(line + half, hist_steps, stride=lines), :]
+        for side in range(2):
+            for piece, (kept, first, count) in enumerate(pieces_of):
+                source = pl.ds(first * lines + side * half + line, count, stride=lines)
+                kept[0][side, k * count : (k + 1) * count, :] = past_ref[source, :]
     pl.semaphore_wait(barrier, areas + group + 2)
 
     def send(src, dst, ssem, rsem, to):
@@ -150,16 +157,21 @@
             src_ref=src, dst_ref=dst, send_sem=ssem, recv_sem=rsem, device_id=to, device_id_type=MESH
         )
 
-    wave_sends = []
-    edge = NEAR * hist_steps
-    for side, way in enumerate((1, -1)):
-        for reach, slots in ((1, pl.ds(0, edge)), (2, pl.ds(edge, half * hist_steps - edge))):
-            sem = 2 * side + reach - 1
-            copy = send(
-                sorted_out.at[side, slots, :], sorted_in.at[side, slots, :], ws.at[sem], wr.at[sem], subnet(way * reach)
-            )
-            copy.start()
-            wave_sends.append(copy)
+    def wave_send(piece):
+        (out, into), _, count = pieces_of[piece]
+        copies = []
+        for side, way in enumerate((1, -1)):
+            for reach, slots in ((1, pl.ds(0, NEAR * count)), (2, pl.ds(NEAR * count, (half - NEAR) * count))):
+                sem = (piece, 2 * side + reach - 1)
+                copy = send(
+                    out.at[side, slots, :], into.at[side, slots, :], ws.at[sem], wr.at[sem], subnet(way * reach)
+                )
+                copy.start()
+                copies.append(copy)
+        return copies
+
+    early_sends = wave_send(0)
+    late_sends = wave_send(1)
 
     def mate(e):
         return zi * inner + lax.rem(xi + e, inner)
@@ -236,12 +248,18 @@
     live = lax.broadcasted_iota(jnp.int32, (convs, 128), 0) < count_ref[0]
     xs[lines + convs + ports :, :] = jnp.zeros((probes - lines - convs - ports, 128), F32)
 
-    def step(t, carry):
+    def advance(both, t, carry):
         cosine = trig_ref[0, t]
         sine = trig_ref[1, t]
-        for l in range(half):
-            xs[l : l + 1, :] = sorted_in[1, pl.ds(base_ref[l] + t, 1), :]
-            xs[l + half : l + half + 1, :] = sorted_in[0, pl.ds(base_ref[l + half] + t, 1), :]
+        for l in range(lines):
+            side = 1 if l < half else 0
+            slot = base_ref[0, l]
+            when = base_ref[1, l] + t
+            row = in_early[side, pl.ds(slot * EARLY + jnp.minimum(when, EARLY - 1), 1), :]
+            if both:
+                other = in_late[side, pl.ds(slot * late + jnp.maximum(when - EARLY, 0), 1), :]
+                row = jnp.where(when < EARLY, row, other)
+            xs[l : l + 1, :] = row
         inward = xs[0:lines, :]
         axial = state_out_ref[0]
         normal = state_out_ref[1]
@@ -279,11 +297,14 @@
         put_state(after)
         return carry
 
-    for copy in wave_sends:
+    for copy in early_sends:
         copy.wait()
-
+    at = EARLY - hist_steps + STEPS
+    lax.fori_loop(0, at, functools.partial(advance, False), 0)
+    for copy in late_sends:
+        copy.wait()
+    step = functools.partial(advance, True)
     stops = [STEPS * 9 // 10 - (pieces - 1 - p) * STEPS * 2 // 5 for p in range(pieces)]
-    at = 0
     for p, stop in enumerate(stops):
         lax.fori_loop(at, stop, step, 0)
         relay_z(p)
@@ -412,10 +433,10 @@
                         send(block, block, xf.at[side, d, e, k], xr.at[plane, x, k], (mate(e), r)).wait_recv()
                     emit(plane, x, chunk, olocal.at[side, d, e]).start()
 
-    members = port_bus_ref.shape[0] // group
+    members = port_bus_ref.shape[1]
     for j in range(group):
         for p in range(members):
-            place = port_bus_ref[j * members + p] - r * bus_ref.shape[1]
+            place = port_bus_ref[j, p] - r * bus_ref.shape[1]
             inside = (place >= 0) & (place < bus_ref.shape[1])
             place = jnp.clip(place, 0, bus_ref.shape[1] - 1)
             for part in range(2):
@@ -544,11 +565,13 @@
             pltpu.VMEM((group, 2, ports, cases), F32),
             pltpu.SemaphoreType.DMA((group,)),
             pltpu.SemaphoreType.DMA((group,)),
-            pltpu.VMEM((2, lines // 2 * steps_kept, cases), F32),
-            pltpu.VMEM((2, lines // 2 * steps_kept, cases), F32),
-            pltpu.SMEM((lines,), jnp.int32),
-            pltpu.SemaphoreType.DMA((4,)),
-            pltpu.SemaphoreType.DMA((4,)),
+            pltpu.VMEM((2, lines // 2 * EARLY, cases), F32),
+            pltpu.VMEM((2, lines // 2 * (steps_kept - EARLY), cases), F32),
+            pltpu.VMEM((2, lines // 2 * EARLY, cases), F32),
+            pltpu.VMEM((2, lines // 2 * (steps_kept - EARLY), cases), F32),
+            pltpu.SMEM((2, lines), jnp.int32),
+            pltpu.SemaphoreType.DMA((2, 4)),
+            pltpu.SemaphoreType.DMA((2, 4)),
         ],
         compiler_params=pltpu.CompilerParams(collective_id=0, has_side_effects=True),
         cost_estimate=pl.CostEstimate(flops=flops, bytes_accessed=8_000_000, transcendentals=0),
@@ -572,7 +595,7 @@
         conv_state[0],
         conv_reference[0],
         port_voltage_prev[:, 0],
-        port_bus.reshape(-1),
+        port_bus,
         zc,
     )
 

time: 136 us -> 131 us (0.963)
  Pallas kernels: 122 us -> 118 us
    pallas_call x1, Pallas kernels: 122 us -> 118 us  [per_device(): pl.pallas_call(functools.partial(window_kernel, lines, convs, ports), out...]
where the time goes in v3:
time: 131 us
  Pallas kernels  118 us (90%)
  local copies, waits for them, and re-layouts  10.9 us (8%)
    pallas_call x1, Pallas kernels, per_device(): pl.pallas_call(functools.partial(window_kernel, lines, convs, ports), out...  118 us
    unnamed x7, local copies, waits for them, and re-layouts  10.9 us

profile of v3, /device:TPU:0, one launch (start us, length us, event | category | flops | bytes accessed | tf_op | source)
XLA Modules:
  0.0 130.6 jit_solution(9453357500521091336)
XLA Ops:
  1.3 118.4 %window.1 = (f32[20,32,128]{2,1,0:T(8,128)}, f32[1024,128]{1,0:T(8,128)}, f32[2,64,128]{2,1,0:T(8,128)}, f32[2,8,128]{2,1,0:T(8,128)}, f32[2,5120,128]{2,1,0:T(8,128)}) custom-call(s32[32]{0:T(128)} %bitcast.28, s32[32]{0:T(128)} %bitcast.29, f32[2,20]{1,0:T(2,128)} %constant.1.clone.trig_ref, s32[1]{0:T(128)S(6)} %copy.31.count_ref, s32[1,32]{1,0:T(1,128)} %line_node_ref.1, ...), custom_call_target="tpu_custom_call" | custom-call | flops 27179089920 | bytes 8000000 | tf_op jit(solution)/shard_map/window/pallas_call | solution.py:526
  119.7 1.7 %copy.32 = f32[1,20,32,128]{3,2,1,0:T(8,128)} copy(f32[1,20,32,128]{3,2,1,0:T(8,128)} %bitcast.18) | data formatting | bytes 655360
  121.4 1.9 %copy.33 = f32[1,1024,128]{2,1,0:T(8,128)} copy(f32[1,1024,128]{2,1,0:T(8,128)} %bitcast.17) | data formatting | bytes 1048576
  123.3 1.5 %copy.34 = f32[1,2,64,128]{3,2,1,0:T(8,128)} copy(f32[1,2,64,128]{3,2,1,0:T(8,128)} %bitcast.19) | data formatting | bytes 131072
  124.8 0.0 copy-start
  124.8 5.2 %copy.35 = f32[2,5120,128]{2,1,0:T(8,128)} copy(f32[2,5120,128]{2,1,0:T(8,128)} %get-tuple-element.28) | data formatting | bytes 10485760
  130.0 0.0 copy-done
  130.0 0.6 copy.36
Async XLA Ops:
  124.8 5.2 %copy-start = (f32[2,8,128]{2,1,0:T(8,128)S(1)}, f32[2,8,128]{2,1,0:T(8,128)}, u32[]{:S(2)}) copy-start(f32[2,8,128]{2,1,0:T(8,128)} %get-tuple-element.14) | copy-start | bytes 24580

commit v4 on v3

--- a/solution.py
+++ b/solution.py
@@ -15,8 +15,11 @@
 BF16 = jnp.bfloat16
 MESH = pl.DeviceIdType.MESH
 SUBS = 10
+BLOCKS = 10
 NEAR = 12
 EARLY = 24
+FIRST = (0, 1, 14)
+REST = (11, 13, 2, 3, 4, 5, 6, 7, 8, 9, 10, 12, 15, 16, 17, 18)
 
 
 def split(x):
@@ -36,25 +39,7 @@
     lines,
     convs,
     ports,
-    partner_ref,
-    delay_ref,
-    trig_ref,
-    count_ref,
-    line_node_ref,
-    conv_node_ref,
-    port_node_ref,
-    line_adm_ref,
-    conv_rate_ref,
-    conv_limit_ref,
-    port_adm_ref,
-    ginv_ref,
-    gcap_ref,
-    hist_ref,
-    past_ref,
-    state_ref,
-    target_ref,
-    pvolt_ref,
-    port_bus_ref,
+    far,
     zc_ref,
     waves_ref,
     hist_out_ref,
@@ -98,7 +83,33 @@
     base_ref,
     ws,
     wr,
+    held,
+    hs,
 ):
+    loads = [pltpu.make_async_copy(there, here, hs.at[i]) for i, (there, here) in enumerate(zip(far, held))]
+    for i in FIRST + REST:
+        loads[i].start()
+    (
+        partner_ref,
+        delay_ref,
+        trig_ref,
+        count_ref,
+        line_node_ref,
+        conv_node_ref,
+        port_node_ref,
+        line_adm_ref,
+        conv_rate_ref,
+        conv_limit_ref,
+        port_adm_ref,
+        ginv_ref,
+        gcap_ref,
+        hist_ref,
+        past_ref,
+        state_ref,
+        target_ref,
+        pvolt_ref,
+        port_bus_ref,
+    ) = held
     nodes = ginv_ref.shape[0]
     probes = 128
     half = lines // 2
@@ -127,6 +138,8 @@
         pl.semaphore_signal(barrier, inc=1, device_id=subnet(by), device_id_type=MESH)
 
     hist_steps = past_ref.shape[0] // lines
+    for i in FIRST:
+        loads[i].wait()
     late = hist_steps - EARLY
     pieces_of = (((out_early, in_early), 0, EARLY), ((out_late, in_late), EARLY, late))
     near = []
@@ -205,6 +218,8 @@
                 copy.start()
                 z_sends.append(copy)
 
+    for i in REST:
+        loads[i].wait()
     pad = probes - lines - convs - ports
 
     def stacked(line, conv, port, rest):
@@ -479,8 +494,47 @@
     return pl.BlockSpec(memory_space=pltpu.VMEM)
 
 
-def smem():
-    return pl.BlockSpec(memory_space=pltpu.SMEM)
+def emit_kernel(count, *refs):
+    sources, targets = refs[:count], refs[count : 2 * count]
+    held, sems, out_sems = refs[2 * count : 3 * count], refs[3 * count], refs[3 * count + 1]
+    loads, stores = [], []
+    for i in range(count):
+        extent = sources[i].shape[0]
+        cuts = BLOCKS if i == count - 1 else 1
+        for k in range(cuts):
+            rows = pl.ds(k * (extent // cuts), extent // cuts)
+            slot = i + k
+            loads.append(pltpu.make_async_copy(sources[i].at[rows], held[i].at[rows], sems.at[slot]))
+            stores.append(pltpu.make_async_copy(held[i].at[rows], targets[i].at[rows], out_sems.at[slot]))
+    order = list(range(count - 1, len(loads))) + list(range(count - 1))
+    for n in order:
+        loads[n].start()
+    for n in order:
+        loads[n].wait()
+        stores[n].start()
+    for n in order:
+        stores[n].wait()
+
+
+def emit_all(*arrays):
+    flat = [x.reshape(-1, x.shape[-1]) for x in arrays]
+    count = len(flat)
+    slots = count - 1 + BLOCKS
+    shapes = [jax.ShapeDtypeStruct(x.shape, x.dtype) for x in flat]
+    done = pl.pallas_call(
+        functools.partial(emit_kernel, count),
+        out_shape=tuple(shapes),
+        in_specs=[pl.BlockSpec(memory_space=pl.ANY)] * count,
+        out_specs=(pl.BlockSpec(memory_space=pl.ANY),) * count,
+        scratch_shapes=[pltpu.VMEM(x.shape, x.dtype) for x in flat]
+        + [pltpu.SemaphoreType.DMA((slots,)), pltpu.SemaphoreType.DMA((slots,))],
+        name="emit",
+    )(*flat)
+    return [y.reshape(x.shape) for x, y in zip(arrays, done)]
+
+
+def hbm():
+    return pl.BlockSpec(memory_space=pltpu.HBM)
 
 
 def per_device(
@@ -523,6 +577,31 @@
     angles = np.arange(1, STEPS + 1, dtype=np.float32) * np.float32(2.0 * math.pi / STEPS)
     trig = jnp.asarray(np.stack([np.cos(angles), np.sin(angles)]).astype(np.float32))
     flops = 2 * STEPS * (nodes + 128) * (2 * nodes + 256) * 256
+    inputs = [
+        line_partner[0],
+        line_delay[0],
+        trig,
+        conv_count,
+        line_node,
+        conv_node,
+        port_node,
+        line_admittance,
+        conv_rate,
+        conv_limit,
+        port_admittance,
+        conductance_inverse[0],
+        cap_conductance,
+        cap_history[0],
+        wave_history.reshape(steps_kept * lines, cases),
+        conv_state[0],
+        conv_reference[0],
+        port_voltage_prev[:, 0],
+        port_bus,
+    ]
+    scalars = (0, 1, 2, 3, len(inputs) - 1)
+    held = [
+        (pltpu.SMEM if i in scalars else pltpu.VMEM)(x.shape, x.dtype) for i, x in enumerate(inputs)
+    ]
     waves, hist_end, conv_out, port_voltage, bus_voltage = pl.pallas_call(
         functools.partial(window_kernel, lines, convs, ports),
         out_shape=(
@@ -532,7 +611,7 @@
             jax.ShapeDtypeStruct((2, ports, cases), F32),
             jax.ShapeDtypeStruct((2, bus_rows, cases), F32),
         ),
-        in_specs=[smem()] * 4 + [vmem()] * 14 + [smem(), pl.BlockSpec(memory_space=pl.ANY)],
+        in_specs=[[hbm()] * len(inputs), hbm()],
         out_specs=(vmem(),) * 4 + (pl.BlockSpec(memory_space=pl.ANY),),
         scratch_shapes=[
             pltpu.VMEM((nodes + 128, 2 * nodes + 256), BF16),
@@ -572,33 +651,18 @@
             pltpu.SMEM((2, lines), jnp.int32),
             pltpu.SemaphoreType.DMA((2, 4)),
             pltpu.SemaphoreType.DMA((2, 4)),
+            held,
+            pltpu.SemaphoreType.DMA((len(inputs),)),
         ],
         compiler_params=pltpu.CompilerParams(collective_id=0, has_side_effects=True),
         cost_estimate=pl.CostEstimate(flops=flops, bytes_accessed=8_000_000, transcendentals=0),
         name="window",
     )(
-        line_partner[0],
-        line_delay[0],
-        trig,
-        conv_count,
-        line_node,
-        conv_node,
-        port_node,
-        line_admittance,
-        conv_rate,
-        conv_limit,
-        port_admittance,
-        conductance_inverse[0],
-        cap_conductance,
-        cap_history[0],
-        wave_history.reshape(steps_kept * lines, cases),
-        conv_state[0],
-        conv_reference[0],
-        port_voltage_prev[:, 0],
-        port_bus,
+        inputs,
         zc,
     )
 
+    waves, hist_end, conv_out, port_voltage, bus_voltage = emit_all(waves, hist_end, conv_out, port_voltage, bus_voltage)
     return (waves[None], hist_end[None], conv_out[None], bus_voltage, port_voltage[:, None])
 
 

time: 131 us -> 123 us (0.939)
  local copies, waits for them, and re-layouts: 10.9 us -> 0 us
  Pallas kernels: 118 us -> 121 us
    unnamed x7 -> x0, local copies, waits for them, and re-layouts: 10.9 us -> none
    pallas_call x0 -> x1, Pallas kernels: none -> 5.45 us  [emit_all(): pl.pallas_call(functools.partial(emit_kernel, count), out_shape=tuple(sha...]
    pallas_call x1, Pallas kernels: 118 us -> 116 us  [per_device(): pl.pallas_call(functools.partial(window_kernel, lines, convs, ports), out...]
where the time goes in v4:
time: 123 us
  Pallas kernels  121 us (98%)
  between operations  1.29 us (1%)
    pallas_call x1, Pallas kernels, per_device(): pl.pallas_call(functools.partial(window_kernel, lines, convs, ports), out...  116 us
    pallas_call x1, Pallas kernels, emit_all(): pl.pallas_call(functools.partial(emit_kernel, count), out_shape=tuple(sha...  5.45 us

profile of v4, /device:TPU:0, one launch (start us, length us, event | category | flops | bytes accessed | tf_op | source)
XLA Modules:
  0.0 122.7 jit_solution(9497354487233002832)
XLA Ops:
  1.3 115.9 %window.1 = (f32[20,32,128]{2,1,0:T(8,128)}, f32[1024,128]{1,0:T(8,128)}, f32[2,64,128]{2,1,0:T(8,128)}, f32[2,8,128]{2,1,0:T(8,128)}, f32[2,5120,128]{2,1,0:T(8,128)}) custom-call(s32[32]{0:T(128)} %bitcast.38, s32[32]{0:T(128)} %bitcast.39, f32[2,20]{1,0:T(2,128)} %constant.1.clone.far_2_, s32[1]{0:T(128)S(6)} %copy.26.far_3_, s32[1,32]{1,0:T(1,128)} %far_4_.1, ...), custom_call_target="tpu_custom_call" | custom-call | flops 27179089920 | bytes 8000000 | tf_op jit(solution)/shard_map/window/pallas_call | solution.py:605
  117.2 5.4 %emit.1 = (f32[640,128]{1,0:T(8,128)}, f32[1024,128]{1,0:T(8,128)}, f32[128,128]{1,0:T(8,128)}, f32[16,128]{1,0:T(8,128)}, f32[10240,128]{1,0:T(8,128)}) custom-call(f32[640,128]{1,0:T(8,128)} %bitcast.23, f32[1024,128]{1,0:T(8,128)} %get-tuple-element.16.refs_1_, f32[128,128]{1,0:T(8,128)} %bitcast.24, f32[16,128]{1,0:T(8,128)} %bitcast.25, ...), custom_call_target="tpu_custom_call" | custom-call | tf_op jit(solution)/shard_map/emit/pallas_call | solution.py:524

commit v5 on v4

--- a/solution.py
+++ b/solution.py
@@ -358,8 +358,6 @@
 
     for p in range(pieces):
         own_z[p].wait()
-    for copy in z_sends:
-        copy.wait_send()
     for p in range(pieces):
         for e in range(1, inner):
             for q in range(outer):
@@ -481,6 +479,8 @@
         up, down = launch(k)
         pl.when(can_up)(up.wait_send)
         pl.when(can_down)(down.wait_send)
+    for copy in z_sends:
+        copy.wait_send()
     for d in range(1, group):
         hand(d).wait()
     value = picked[r]

time: 123 us -> 123 us (level)
  no operation moved by 1% of the time
where the time goes in v5:
time: 123 us
  Pallas kernels  121 us (98%)
  between operations  1.29 us (1%)
    pallas_call x1, Pallas kernels, per_device(): pl.pallas_call(functools.partial(window_kernel, lines, convs, ports), out...  116 us
    pallas_call x1, Pallas kernels, emit_all(): pl.pallas_call(functools.partial(emit_kernel, count), out_shape=tuple(sha...  5.45 us

profile of v5, /device:TPU:0, one launch (start us, length us, event | category | flops | bytes accessed | tf_op | source)
XLA Modules:
  0.0 122.6 jit_solution(10403452632927156631)
XLA Ops:
  1.3 115.9 %window.1 = (f32[20,32,128]{2,1,0:T(8,128)}, f32[1024,128]{1,0:T(8,128)}, f32[2,64,128]{2,1,0:T(8,128)}, f32[2,8,128]{2,1,0:T(8,128)}, f32[2,5120,128]{2,1,0:T(8,128)}) custom-call(s32[32]{0:T(128)} %bitcast.38, s32[32]{0:T(128)} %bitcast.39, f32[2,20]{1,0:T(2,128)} %constant.1.clone.far_2_, s32[1]{0:T(128)S(6)} %copy.26.far_3_, s32[1,32]{1,0:T(1,128)} %far_4_.1, ...), custom_call_target="tpu_custom_call" | custom-call | flops 27179089920 | bytes 8000000 | tf_op jit(solution)/shard_map/window/pallas_call | solution.py:605
  117.2 5.4 %emit.1 = (f32[640,128]{1,0:T(8,128)}, f32[1024,128]{1,0:T(8,128)}, f32[128,128]{1,0:T(8,128)}, f32[16,128]{1,0:T(8,128)}, f32[10240,128]{1,0:T(8,128)}) custom-call(f32[640,128]{1,0:T(8,128)} %bitcast.23, f32[1024,128]{1,0:T(8,128)} %get-tuple-element.16.refs_1_, f32[128,128]{1,0:T(8,128)} %bitcast.24, f32[16,128]{1,0:T(8,128)} %bitcast.25, ...), custom_call_target="tpu_custom_call" | custom-call | tf_op jit(solution)/shard_map/emit/pallas_call | solution.py:524
